TPU v7x, 32 devices: a whole 2x2x4 slice. The times are simulated.
32 devices in a mesh: scan: 8 (over y, x, core), tile: 4 (over z).
Axes of the slice: x: 2, y: 2, z: 4, core: 2. Of those that a mesh axis runs over, the one named last changes fastest.
Arguments:
- object_field: float32 [2, 2048, 1024], P(None, 'scan', 'tile'), may hold values from -4.2 to 4.2
- probe_modes: float32 [8, 2, 256, 256], P('tile'), may hold values from -2.1 to 2.1
- amplitudes: bfloat16 [64, 256, 256], P('scan'), may hold values from 0.25 to 3
- positions: int32 [64, 2], P('scan'), may hold values from 0 to 1792, as said below
- counts: int32 [8], P('scan'), may hold values from 1 to 8, as said below
Outputs:
- new_object: float32 [2, 2048, 1024], P(None, 'scan', 'tile')
- probe_step: float32 [8, 2, 256, 256], P('tile')
Inputs may be any that keep to these rules, and one draw needn't show every extreme that they name: `positions`: slot j's row offset lies in rows (j // 8) * 256 to (j // 8) * 256 + 255; every window lies inside the object: row offsets at most 1792, column offsets at most 768. `counts`: some scan index holds 8 live slots and some holds one.
All inputs are finite; a program needn't handle non-finite values.
Results may differ from a plain program's by a relative error of at most 0.003.
Values may be sent and summed in bfloat16 or wider, within the bound.
No kernel may reach another device: no remote copies, remote signals or barrier semaphores. Data moves between devices by JAX's collectives and lax.ppermute only.
A program may use at most 128 MiB of HBM per device.

v0:
```python
import math
import jax
import jax.numpy as jnp
from jax import lax
from jax.sharding import PartitionSpec as P

damping = 1.0
amp_floor = 0.5


def passed_along(value, axis, steps):
    count = lax.axis_size(axis)
    leading, last = (max(0, -steps), min(count, count - steps))
    return lax.ppermute(value, axis, [(source, source + steps) for source in range(leading, last)])


def dft_tables(win_width):
    index_row = jnp.arange(win_width, dtype=jnp.int32)
    products = index_row[:, None] * index_row[None, :] % win_width
    phase_angle = products.astype(jnp.float32) * (2.0 * math.pi / win_width)
    norm_scale = 1.0 / math.sqrt(win_width)
    real_part = (jnp.cos(phase_angle) * norm_scale).astype(jnp.bfloat16)
    imag_part = (-jnp.sin(phase_angle) * norm_scale).astype(jnp.bfloat16)
    return (real_part, imag_part)


def transform(rowform, right_table, left_table, win_width):
    half_done = jnp.einsum(
        "mak,kl->mal", rowform, right_table, preferred_element_type=jnp.float32
    ).astype(jnp.bfloat16)
    full_block = jnp.einsum(
        "ca,mak->mck", left_table, half_done, preferred_element_type=jnp.float32
    )
    real_out = full_block[..., :win_width, :win_width] - full_block[..., win_width:, win_width:]
    imag_out = full_block[..., :win_width, win_width:] + full_block[..., win_width:, :win_width]
    return (real_out, imag_out)


def shards(object_field, probe_modes, amplitudes, positions, counts):
    slot_count = amplitudes.shape[0]
    win_width = amplitudes.shape[1]
    band_rows = object_field.shape[1]
    first_row = lax.axis_index("scan") * band_rows
    object_low = object_field.astype(jnp.bfloat16)
    lower_rows = passed_along(object_low, "scan", -1)
    extended = jnp.concatenate([object_low, lower_rows], axis=1)
    band_all = lax.all_gather(extended, "tile", axis=2, tiled=True)
    row_offsets = positions[:, 0] - first_row
    col_offsets = positions[:, 1]
    zero_index = jnp.zeros((), jnp.int32)

    def cut_window(row_at, col_at):
        return lax.dynamic_slice(band_all, (zero_index, row_at, col_at), (2, win_width, win_width))

    windows = jax.vmap(cut_window)(row_offsets, col_offsets)
    slot_ids = jnp.arange(slot_count, dtype=jnp.int32)
    live_mask = (slot_ids < counts[0]).astype(jnp.float32)
    real_part, imag_part = dft_tables(win_width)
    right_fwd = jnp.block([[real_part, imag_part], [-imag_part, real_part]])
    left_fwd = jnp.concatenate([real_part, imag_part], axis=0)
    right_inv = jnp.block([[real_part, -imag_part], [imag_part, real_part]])
    left_inv = jnp.concatenate([real_part, -imag_part], axis=0)
    probe_re = probe_modes[:, 0]
    probe_im = probe_modes[:, 1]
    probe_power = jnp.sum(probe_re * probe_re + probe_im * probe_im, axis=0)

    def forward_one(window):
        window_re = window[0].astype(jnp.float32)
        window_im = window[1].astype(jnp.float32)
        exit_wave = jnp.concatenate(
            [
                probe_re * window_re - probe_im * window_im,
                probe_re * window_im + probe_im * window_re,
            ],
            axis=-1,
        ).astype(jnp.bfloat16)
        far_re, far_im = transform(exit_wave, right_fwd, left_fwd, win_width)
        return (far_re, far_im, jnp.sum(far_re * far_re + far_im * far_im, axis=0))

    far_re, far_im, local_power = lax.map(forward_one, windows)
    intensity = lax.psum(local_power, "tile")
    factor = live_mask[:, None, None] * (
        amplitudes.astype(jnp.float32) / jnp.maximum(jnp.sqrt(intensity), amp_floor) - 1.0
    )
    channels = 3

    def accumulate(running, inputs):
        buffer, grad_sum, weight_sum = running
        slot_re, slot_im, slot_factor, window, live, row_at, col_at = inputs
        change = jnp.concatenate([slot_factor * slot_re, slot_factor * slot_im], axis=-1).astype(
            jnp.bfloat16
        )
        near_re, near_im = transform(change, right_inv, left_inv, win_width)
        window_re = window[0].astype(jnp.float32)
        window_im = window[1].astype(jnp.float32)
        numer_parts = [
            jnp.sum(probe_re * near_re + probe_im * near_im, axis=0),
            jnp.sum(probe_re * near_im - probe_im * near_re, axis=0),
        ]
        numer_parts.append(live * probe_power)
        numer = jnp.stack(numer_parts)
        grads = jnp.stack(
            [window_re * near_re + window_im * near_im, window_re * near_im - window_im * near_re],
            axis=1,
        )
        weight = window_re * window_re + window_im * window_im
        region = lax.dynamic_slice(
            buffer, (zero_index, row_at, col_at), (channels, win_width, win_width)
        )
        buffer = lax.dynamic_update_slice(buffer, region + numer, (zero_index, row_at, col_at))
        return ((buffer, grad_sum + grads, weight_sum + live * weight), None)

    init = (
        jnp.zeros((channels, band_rows + win_width, band_all.shape[2]), jnp.float32),
        jnp.zeros(probe_modes.shape, jnp.float32),
        jnp.zeros((win_width, win_width), jnp.float32),
    )
    (buffer, grad_sum, weight_sum), _ = lax.scan(
        accumulate, init, (far_re, far_im, factor, windows, live_mask, row_offsets, col_offsets)
    )
    rim_rows = passed_along(buffer[:, band_rows:, :].astype(jnp.bfloat16), "scan", 1).astype(
        jnp.float32
    )
    own_rows = buffer[:, :band_rows, :].at[:, :win_width, :].add(rim_rows)
    totals = lax.psum_scatter(own_rows, "tile", scatter_dimension=2, tiled=True)
    illumination = totals[2]
    new_object = object_field + totals[0:2] / (illumination + damping)[None]
    grad_total, weight_total = lax.psum((grad_sum, weight_sum), "scan")
    probe_step = grad_total / (weight_total + damping)[None, None]
    return (new_object, probe_step)


def solution(mesh):
    placed = (
        P(None, "scan", "tile"),
        P("tile", None, None, None),
        P("scan", None, None),
        P("scan", None),
        P("scan"),
    )
    return jax.shard_map(
        shards,
        mesh=mesh,
        in_specs=placed,
        out_specs=(P(None, "scan", "tile"), P("tile", None, None, None)),
        check_vma=False,
    )
```

profile of v0, /device:TPU:0, one launch (start us, length us, event | category | flops | bytes accessed | tf_op | source)
XLA Modules:
  0.0 640.8 jit_solution(17734044107008832897)
XLA Ops:
  18.0 47.6 %all-gather.2.cloned.1.call-done = bf16[2,512,1024]{2,1,0:T(8,128)(2,1)} async-done(((bf16[2,512,256]{2,1,0:T(8,128)(2,1)}), bf16[2,512,1024]{2,1,0:T(8,128)(2,1)}) %all-gather.2.cloned.1.call-update) | async-done | bytes 2097168 | tf_op jit(solution)/shard_map/all_gather | solution.py:47
  65.5 30.1 %while.33 = (s32[]{:T(128)}, bf16[2,512,1024]{2,1,0:T(8,128)(2,1)}, s32[8,3]{0,1:T(4,128)S(1)}, bf16[8,2,256,256]{3,2,1,0:T(8,128)(2,1)}, s32[]{:T(128)}) while((s32[]{:T(128)}, bf16[2,512,1024]{2,1,0:T(8,128)(2,1)}, s32[8,3]{0,1:T(4,128)S(1)}, bf16[8,2,256,256]{3,2,1,0:T(8,128)(2,1)}, s32[]{:T(128)}) %tuple.102), condition=%wide.while_cond.1, body=%wide.while_body.1.sunk | while | flops 2 | bytes 525429 | solution.py:53
  66.1 3.2 bitcast_dynamic-update-slice_fusion.6
  73.6 3.2 bitcast_dynamic-update-slice_fusion.6
  77.4 3.2 bitcast_dynamic-update-slice_fusion.6
  81.2 3.2 bitcast_dynamic-update-slice_fusion.6
  92.5 3.2 bitcast_dynamic-update-slice_fusion.6
  95.7 42.0 %while.32 = (s32[]{:T(128)}, f32[8,2,256,256]{2,3,1,0:T(8,128)}, f32[8,2,256,256]{2,3,1,0:T(8,128)}, f32[8,256,256]{2,1,0:T(8,128)}, bf16[8,2,256,256]{3,2,1,0:T...) while((s32[]{:T(128)}, f32[8,2,256,256]{2,3,1,0:T(8,128)}, ...), condition=%wide.region_2.3_spmd, body=%wide.region_0.2_spmd.sunk | while | flops 540344320 | bytes 12845209 | solution.py:80
  142.9 79.3 %all-reduce.4.cloned.1.call-done = f32[8,256,256]{2,1,0:T(8,128)} async-done(((f32[8,256,256]{2,1,0:T(8,128)}), f32[8,256,256]{2,1,0:T(8,128)}) %all-reduce.4.cloned.1.call-update) | async-done | bytes 2097168 | tf_op jit(solution)/shard_map/psum | solution.py:81
  222.2 3.8 add_multiply_fusion
  226.0 3.5 broadcast_in_dim.23.clone
  229.4 267.6 %while.34 = (s32[]{:T(128)}, f32[3,512,1024]{2,1,0:T(8,128)}, f32[2,2,256,256]{2,3,0,1:T(8,128)}, f32[256,256]{0,1:T(8,128)}, s32[8]{0:T(128)S(1)}, /*index=5*/s...) while((s32[]{:T(128)}, f32[3,512,1024]{2,1,0:T(8,128)}, ...), condition=%wide.region_8.9_spmd.clone, body=%wide.region_5.8_spmd.clone.sunk | while | flops 542769152 | bytes 35914140 | solution.py:118
  252.2 8.3 %dynamic_update_slice.23 = f32[3,512,1024]{2,1,0:T(8,128)} dynamic-update-slice(f32[3,512,1024]{2,1,0:T(8,128)} %get-tuple-element.660, f32[3,256,256]{2,1,0:T(8,128)S(1)} %copy.58, s32[]{:T(128)} %constant.100.clone.1..sunk.1, s32[]{:T(128)S(6)} %select_n.65, s32[]{:T(128)S(6)} %select_n.66) | dynamic-update-slice | bytes 1572868 | tf_op jit(solution)/shard_map/while/body/eval_jaxpr/dynamic_update_slice | solution.py:110
  285.3 7.4 %dynamic_update_slice.23 = f32[3,512,1024]{2,1,0:T(8,128)} dynamic-update-slice(f32[3,512,1024]{2,1,0:T(8,128)} %get-tuple-element.660, f32[3,256,256]{2,1,0:T(8,128)S(1)} %copy.58, s32[]{:T(128)} %constant.100.clone.1..sunk.1, s32[]{:T(128)S(6)} %select_n.65, s32[]{:T(128)S(6)} %select_n.66) | dynamic-update-slice | bytes 1572868 | tf_op jit(solution)/shard_map/while/body/eval_jaxpr/dynamic_update_slice | solution.py:110
  317.7 9.4 %dynamic_update_slice.23 = f32[3,512,1024]{2,1,0:T(8,128)} dynamic-update-slice(f32[3,512,1024]{2,1,0:T(8,128)} %get-tuple-element.660, f32[3,256,256]{2,1,0:T(8,128)S(1)} %copy.58, s32[]{:T(128)} %constant.100.clone.1..sunk.1, s32[]{:T(128)S(6)} %select_n.65, s32[]{:T(128)S(6)} %select_n.66) | dynamic-update-slice | bytes 1572868 | tf_op jit(solution)/shard_map/while/body/eval_jaxpr/dynamic_update_slice | solution.py:110
  352.0 8.7 %dynamic_update_slice.23 = f32[3,512,1024]{2,1,0:T(8,128)} dynamic-update-slice(f32[3,512,1024]{2,1,0:T(8,128)} %get-tuple-element.660, f32[3,256,256]{2,1,0:T(8,128)S(1)} %copy.58, s32[]{:T(128)} %constant.100.clone.1..sunk.1, s32[]{:T(128)S(6)} %select_n.65, s32[]{:T(128)S(6)} %select_n.66) | dynamic-update-slice | bytes 1572868 | tf_op jit(solution)/shard_map/while/body/eval_jaxpr/dynamic_update_slice | solution.py:110
  385.6 8.8 %dynamic_update_slice.23 = f32[3,512,1024]{2,1,0:T(8,128)} dynamic-update-slice(f32[3,512,1024]{2,1,0:T(8,128)} %get-tuple-element.660, f32[3,256,256]{2,1,0:T(8,128)S(1)} %copy.58, s32[]{:T(128)} %constant.100.clone.1..sunk.1, s32[]{:T(128)S(6)} %select_n.65, s32[]{:T(128)S(6)} %select_n.66) | dynamic-update-slice | bytes 1572868 | tf_op jit(solution)/shard_map/while/body/eval_jaxpr/dynamic_update_slice | solution.py:110
  419.4 9.2 %dynamic_update_slice.23 = f32[3,512,1024]{2,1,0:T(8,128)} dynamic-update-slice(f32[3,512,1024]{2,1,0:T(8,128)} %get-tuple-element.660, f32[3,256,256]{2,1,0:T(8,128)S(1)} %copy.58, s32[]{:T(128)} %constant.100.clone.1..sunk.1, s32[]{:T(128)S(6)} %select_n.65, s32[]{:T(128)S(6)} %select_n.66) | dynamic-update-slice | bytes 1572868 | tf_op jit(solution)/shard_map/while/body/eval_jaxpr/dynamic_update_slice | solution.py:110
  453.5 9.1 %dynamic_update_slice.23 = f32[3,512,1024]{2,1,0:T(8,128)} dynamic-update-slice(f32[3,512,1024]{2,1,0:T(8,128)} %get-tuple-element.660, f32[3,256,256]{2,1,0:T(8,128)S(1)} %copy.58, s32[]{:T(128)} %constant.100.clone.1..sunk.1, s32[]{:T(128)S(6)} %select_n.65, s32[]{:T(128)S(6)} %select_n.66) | dynamic-update-slice | bytes 1572868 | tf_op jit(solution)/shard_map/while/body/eval_jaxpr/dynamic_update_slice | solution.py:110
  487.6 9.4 %dynamic_update_slice.23 = f32[3,512,1024]{2,1,0:T(8,128)} dynamic-update-slice(f32[3,512,1024]{2,1,0:T(8,128)} %get-tuple-element.660, f32[3,256,256]{2,1,0:T(8,128)S(1)} %copy.58, s32[]{:T(128)} %constant.100.clone.1..sunk.1, s32[]{:T(128)S(6)} %select_n.65, s32[]{:T(128)S(6)} %select_n.66) | dynamic-update-slice | bytes 1572868 | tf_op jit(solution)/shard_map/while/body/eval_jaxpr/dynamic_update_slice | solution.py:110
  499.2 4.5 collective-permute-start.1
  505.8 4.9 convert_add_fusion
  510.7 58.9 %all-reduce.6.cloned.1.call-done = (f32[2,2,256,256]{3,2,1,0:T(8,128)}, f32[256,256]{0,1:T(8,128)}) async-done(((f32[2,2,256,256]{3,2,1,0:T(8,128)}, f32[256,256]{0,1:T(8,128)}), (f32[2,2,256,256]{3,2,1,0:T(8,128)}, f32[256,256]{0,1:T(8,128)})) %all-reduce.6.cloned.1.call-update) | async-done | bytes 1310736 | tf_op jit(solution)/shard_map/psum | solution.py:128
  573.0 58.3 %reduce-scatter.2.cloned.1.call-done = f32[3,256,256]{2,1,0:T(8,128)} async-done(((f32[3,256,1024]{2,1,0:T(8,128)}), f32[3,256,256]{2,1,0:T(8,128)}) %reduce-scatter.2.cloned.1.call-update) | async-done | bytes 786448 | tf_op jit(solution)/shard_map/reduce_scatter | solution.py:125
  (335 shorter events, 247.6 us)
Async XLA Ops:
  7.2 5.7 copy-start.8
  7.2 58.4 %all-gather.2.cloned.1.call-start = ((), (), s32[]{:S(2)}) async-start(), calls=%async_computation.1 | async-start | bytes 2621440 | tf_op jit(solution)/shard_map/all_gather | solution.py:47
  8.3 8.3 %copy-start.6 = (f32[2,2,256,256]{3,2,1,0:T(8,128)S(1)}, f32[2,2,256,256]{3,2,1,0:T(8,128)}, u32[]{:S(2)}) copy-start(f32[2,2,256,256]{3,2,1,0:T(8,128)} %param.14) | copy-start | bytes 3145732
  8.3 3.6 collective-permute-start
  12.7 209.4 %all-reduce.4.cloned.1.call-start = ((), (), s32[]{:S(2)}) async-start(), calls=%async_computation.2 | async-start | bytes 4194304 | tf_op jit(solution)/shard_map/psum | solution.py:81
  137.6 2.0 copy-start.4
  137.7 84.5 %copy-start.7 = (bf16[8,256,256]{2,1,0:T(8,128)(2,1)S(1)}, bf16[8,256,256]{2,1,0:T(8,128)(2,1)}, u32[]{:S(2)}) copy-start(bf16[8,256,256]{2,1,0:T(8,128)(2,1)} %param.15) | copy-start | bytes 3145732
  137.7 432.0 %all-reduce.6.cloned.1.call-start = ((), (), s32[]{:S(2)}) async-start(), calls=%async_computation.4 | async-start | bytes 2621440 | tf_op jit(solution)/shard_map/psum | solution.py:128
  248.5 1.5 copy-start.2
  250.0 1.0 copy-start
  280.4 1.5 copy-start.2
  312.8 1.5 copy-start.2
  314.3 1.0 copy-start
  347.1 1.5 copy-start.2
  348.6 1.0 copy-start
  380.7 1.5 copy-start.2
  382.3 1.0 copy-start
  414.5 1.5 copy-start.2
  448.6 1.5 copy-start.2
  482.7 1.5 copy-start.2
  497.0 6.8 %copy-start.1 = (f32[2,2,256,256]{2,3,0,1:T(8,128)S(1)}, f32[2,2,256,256]{2,3,0,1:T(8,128)}, u32[]{:S(2)}) copy-start(f32[2,2,256,256]{2,3,0,1:T(8,128)} %get-tuple-element.159) | copy-start | bytes 3145732
  499.2 6.6 %collective-permute-start.1 = (bf16[3,256,1024]{2,1,0:T(8,128)(2,1)S(1)}, bf16[3,256,1024]{2,1,0:T(8,128)(2,1)}, u32[]{:S(2)}, u32[]{:S(2)}) collective-permute-start(bf16[3,256,1024]{2,1,0:T(8,128)(2,1)S(1)} %slice.165), channel_id=1, source_target_pairs={{0,4},{4,8},{8,12},{12,16},{16,20},{20,24},{24,28},{1,5},{5,9},{9,... | collective-permute-start | bytes 4718600 | tf_op jit(solution)/shard_map/ppermute | solution.py:14
  505.1 126.2 %reduce-scatter.2.cloned.1.call-start = ((), (), s32[]{:S(2)}) async-start(), calls=%async_computation.3 | async-start | bytes 3932160 | tf_op jit(solution)/shard_map/reduce_scatter | solution.py:125
  510.7 121.6 %copy-start.3 = (f32[2,256,256]{2,1,0:T(8,128)S(1)}, f32[2,256,256]{2,1,0:T(8,128)}, u32[]{:S(2)}) copy-start(f32[2,256,256]{2,1,0:T(8,128)} %param.13) | copy-start | bytes 1572868
  (5 other events, 5.2 us)
Sparse Core Ops, SparseCore 0:
  12.8 52.6 all-gather.1
  137.8 84.3 all-reduce.3
  505.2 64.3 all-reduce.5
  571.8 59.5 reduce-scatter.1
where the time goes:
time: 647 us; the launch traced here: 641 us
  waiting for transfers between devices  247 us (38%)
  local copies, waits for them, and re-layouts  185 us (29%)
  other arithmetic  134 us (21%)
  loops' own time  31.6 us (5%)
  matrix products  22.2 us (3%)
  between operations  14.7 us (2%)
    psum x1, waiting for transfers between devices, shards(): intensity = lax.psum(local_power, 'tile')  79.3 us
    dynamic_update_slice x16, local copies, waits for them, and re-layouts, accumulate(): lax.dynamic_update_slice(buffer, region + numer, (zero_index, row_at, col...  72.4 us
    psum x1, waiting for transfers between devices, shards(): grad_total, weight_total = lax.psum((grad_sum, weight_sum), 'scan')  58.9 us
    reduce_scatter x1, waiting for transfers between devices, shards(): totals = lax.psum_scatter(own_rows, 'tile', scatter_dimension=2, tiled=True)  58.3 us
    all_gather x1, waiting for transfers between devices, shards(): band_all = lax.all_gather(extended, 'tile', axis=2, tiled=True)  47.6 us
    add x16, other arithmetic, accumulate(): return ((buffer, grad_sum + grads, weight_sum + live * weight), None)  35.4 us
    another operation x1, loops' own time, shards(): lax.scan(accumulate, init, (far_re, far_im, factor, windows, live_mask, r...  31.4 us
    gather x24, local copies, waits for them, and re-layouts  30.1 us
  transfers between devices with their start and end apart: 6, of which 6 were waited for; matrix products, arithmetic and copies ran while one was open for 3% of the time, Pallas kernels for 0%

commit v1 on v0

--- a/solution.py
+++ b/solution.py
@@ -78,7 +78,11 @@
         return (far_re, far_im, jnp.sum(far_re * far_re + far_im * far_im, axis=0))
 
     far_re, far_im, local_power = lax.map(forward_one, windows)
-    intensity = lax.psum(local_power, "tile")
+    intensity = local_power
+    for hop in (1, 2):
+        intensity = intensity + lax.ppermute(
+            intensity, "tile", [(dev, dev ^ hop) for dev in range(4)]
+        )
     factor = live_mask[:, None, None] * (
         amplitudes.astype(jnp.float32) / jnp.maximum(jnp.sqrt(intensity), amp_floor) - 1.0
     )

time: 647 us -> 707 us (1.093)
  waiting for transfers between devices: 247 us -> 299 us
    ppermute x0 -> x2, waiting for transfers between devices: none -> 131 us  [shards(): lax.ppermute(intensity, 'tile', [(dev, dev ^ hop) for dev in range(4)])]
    psum x1 -> x0, waiting for transfers between devices: 79.3 us -> none  [shards(): intensity = lax.psum(local_power, 'tile')]
  transfers between devices with their start and end apart: 6 -> 7, of which waited for: 6 -> 7; matrix products, arithmetic and copies ran while one was open for 3% -> 3% of each run, Pallas kernels for 0% -> 0%
where the time goes in v1:
time: 707 us; the launch traced here: 701 us
  waiting for transfers between devices  299 us (42%)
  local copies, waits for them, and re-layouts  185 us (26%)
  other arithmetic  136 us (19%)
  loops' own time  34.2 us (5%)
  matrix products  22.2 us (3%)
  between operations  14.6 us (2%)
  starting transfers between devices  9.85 us (1%)
    ppermute x2, waiting for transfers between devices, shards(): lax.ppermute(intensity, 'tile', [(dev, dev ^ hop) for dev in range(4)])  131 us
    dynamic_update_slice x16, local copies, waits for them, and re-layouts, accumulate(): lax.dynamic_update_slice(buffer, region + numer, (zero_index, row_at, col...  72.5 us
    psum x1, waiting for transfers between devices, shards(): grad_total, weight_total = lax.psum((grad_sum, weight_sum), 'scan')  59.1 us
    reduce_scatter x1, waiting for transfers between devices, shards(): totals = lax.psum_scatter(own_rows, 'tile', scatter_dimension=2, tiled=True)  58.5 us
    all_gather x1, waiting for transfers between devices, shards(): band_all = lax.all_gather(extended, 'tile', axis=2, tiled=True)  47.6 us
    add x16, other arithmetic, accumulate(): return ((buffer, grad_sum + grads, weight_sum + live * weight), None)  35.8 us
    another operation x1, loops' own time, shards(): lax.scan(accumulate, init, (far_re, far_im, factor, windows, live_mask, r...  34 us
    gather x24, local copies, waits for them, and re-layouts  29.3 us
  transfers between devices with their start and end apart: 7, of which 7 were waited for; matrix products, arithmetic and copies ran while one was open for 3% of the time, Pallas kernels for 0%

profile of v1, /device:TPU:0, one launch (start us, length us, event | category | flops | bytes accessed | tf_op | source)
XLA Modules:
  0.0 701.3 jit_solution(12704562774946881168)
XLA Ops:
  18.0 47.6 %all-gather.2.cloned.1.call-done = bf16[2,512,1024]{2,1,0:T(8,128)(2,1)} async-done(((bf16[2,512,256]{2,1,0:T(8,128)(2,1)}), bf16[2,512,1024]{2,1,0:T(8,128)(2,1)}) %all-gather.2.cloned.1.call-update) | async-done | bytes 2097168 | tf_op jit(solution)/shard_map/all_gather | solution.py:47
  65.5 29.3 %while.33 = (s32[]{:T(128)}, bf16[2,512,1024]{2,1,0:T(8,128)(2,1)}, s32[8,3]{0,1:T(4,128)S(1)}, bf16[8,2,256,256]{3,2,1,0:T(8,128)(2,1)}, s32[]{:T(128)}) while((s32[]{:T(128)}, bf16[2,512,1024]{2,1,0:T(8,128)(2,1)}, s32[8,3]{0,1:T(4,128)S(1)}, bf16[8,2,256,256]{3,2,1,0:T(8,128)(2,1)}, s32[]{:T(128)}) %tuple.102), condition=%wide.while_cond.1, body=%wide.while_body.1.sunk | while | flops 2 | bytes 525429 | solution.py:53
  66.1 3.1 bitcast_dynamic-update-slice_fusion.6
  77.1 3.1 bitcast_dynamic-update-slice_fusion.6
  91.8 3.1 bitcast_dynamic-update-slice_fusion.6
  94.9 41.9 %while.32 = (s32[]{:T(128)}, f32[8,2,256,256]{2,3,1,0:T(8,128)}, f32[8,2,256,256]{2,3,1,0:T(8,128)}, f32[8,256,256]{2,1,0:T(8,128)}, bf16[8,2,256,256]{3,2,1,0:T...) while((s32[]{:T(128)}, f32[8,2,256,256]{2,3,1,0:T(8,128)}, ...), condition=%wide.region_2.3_spmd, body=%wide.region_0.2_spmd.sunk | while | flops 540344320 | bytes 12845209 | solution.py:80
  136.8 46.0 %collective-permute-done.1 = f32[8,256,256]{2,1,0:T(8,128)S(1)} collective-permute-done((f32[8,256,256]{2,1,0:T(8,128)}, f32[8,256,256]{2,1,0:T(8,128)S(1)}, u32[]{:S(2)}, u32[]{:S(2)}) %collective-permute-start.1) | collective-permute-done | bytes 2097184 | tf_op jit(solution)/shard_map/ppermute | solution.py:83
  184.8 3.3 collective-permute-start.2
  192.8 84.6 %collective-permute-done.2 = f32[8,256,256]{2,1,0:T(8,128)} collective-permute-done((f32[8,256,256]{2,1,0:T(8,128)S(1)}, f32[8,256,256]{2,1,0:T(8,128)}, u32[]{:S(2)}, u32[]{:S(2)}) %collective-permute-start.2) | collective-permute-done | bytes 2097184 | tf_op jit(solution)/shard_map/ppermute | solution.py:83
  277.5 4.1 add_multiply_fusion
  281.6 3.4 broadcast_in_dim.23.clone
  285.0 271.7 %while.34 = (s32[]{:T(128)}, f32[3,512,1024]{2,1,0:T(8,128)}, f32[2,2,256,256]{2,3,0,1:T(8,128)}, f32[256,256]{0,1:T(8,128)}, s32[8]{0:T(128)S(1)}, /*index=5*/s...) while((s32[]{:T(128)}, f32[3,512,1024]{2,1,0:T(8,128)}, ...), condition=%wide.region_7.8_spmd.clone, body=%wide.region_4.7_spmd.clone.sunk | while | flops 542769152 | bytes 35914140 | solution.py:122
  308.3 8.4 %dynamic_update_slice.23 = f32[3,512,1024]{2,1,0:T(8,128)} dynamic-update-slice(f32[3,512,1024]{2,1,0:T(8,128)} %get-tuple-element.660, f32[3,256,256]{2,1,0:T(8,128)S(1)} %copy.59, s32[]{:T(128)} %constant.100.clone.1..sunk.1, s32[]{:T(128)S(6)} %select_n.65, s32[]{:T(128)S(6)} %select_n.66) | dynamic-update-slice | bytes 1572868 | tf_op jit(solution)/shard_map/while/body/eval_jaxpr/dynamic_update_slice | solution.py:114
  342.0 7.4 %dynamic_update_slice.23 = f32[3,512,1024]{2,1,0:T(8,128)} dynamic-update-slice(f32[3,512,1024]{2,1,0:T(8,128)} %get-tuple-element.660, f32[3,256,256]{2,1,0:T(8,128)S(1)} %copy.59, s32[]{:T(128)} %constant.100.clone.1..sunk.1, s32[]{:T(128)S(6)} %select_n.65, s32[]{:T(128)S(6)} %select_n.66) | dynamic-update-slice | bytes 1572868 | tf_op jit(solution)/shard_map/while/body/eval_jaxpr/dynamic_update_slice | solution.py:114
  374.8 9.4 %dynamic_update_slice.23 = f32[3,512,1024]{2,1,0:T(8,128)} dynamic-update-slice(f32[3,512,1024]{2,1,0:T(8,128)} %get-tuple-element.660, f32[3,256,256]{2,1,0:T(8,128)S(1)} %copy.59, s32[]{:T(128)} %constant.100.clone.1..sunk.1, s32[]{:T(128)S(6)} %select_n.65, s32[]{:T(128)S(6)} %select_n.66) | dynamic-update-slice | bytes 1572868 | tf_op jit(solution)/shard_map/while/body/eval_jaxpr/dynamic_update_slice | solution.py:114
  409.7 8.7 %dynamic_update_slice.23 = f32[3,512,1024]{2,1,0:T(8,128)} dynamic-update-slice(f32[3,512,1024]{2,1,0:T(8,128)} %get-tuple-element.660, f32[3,256,256]{2,1,0:T(8,128)S(1)} %copy.59, s32[]{:T(128)} %constant.100.clone.1..sunk.1, s32[]{:T(128)S(6)} %select_n.65, s32[]{:T(128)S(6)} %select_n.66) | dynamic-update-slice | bytes 1572868 | tf_op jit(solution)/shard_map/while/body/eval_jaxpr/dynamic_update_slice | solution.py:114
  443.8 8.8 %dynamic_update_slice.23 = f32[3,512,1024]{2,1,0:T(8,128)} dynamic-update-slice(f32[3,512,1024]{2,1,0:T(8,128)} %get-tuple-element.660, f32[3,256,256]{2,1,0:T(8,128)S(1)} %copy.59, s32[]{:T(128)} %constant.100.clone.1..sunk.1, s32[]{:T(128)S(6)} %select_n.65, s32[]{:T(128)S(6)} %select_n.66) | dynamic-update-slice | bytes 1572868 | tf_op jit(solution)/shard_map/while/body/eval_jaxpr/dynamic_update_slice | solution.py:114
  478.1 9.3 %dynamic_update_slice.23 = f32[3,512,1024]{2,1,0:T(8,128)} dynamic-update-slice(f32[3,512,1024]{2,1,0:T(8,128)} %get-tuple-element.660, f32[3,256,256]{2,1,0:T(8,128)S(1)} %copy.59, s32[]{:T(128)} %constant.100.clone.1..sunk.1, s32[]{:T(128)S(6)} %select_n.65, s32[]{:T(128)S(6)} %select_n.66) | dynamic-update-slice | bytes 1572868 | tf_op jit(solution)/shard_map/while/body/eval_jaxpr/dynamic_update_slice | solution.py:114
  512.8 9.2 %dynamic_update_slice.23 = f32[3,512,1024]{2,1,0:T(8,128)} dynamic-update-slice(f32[3,512,1024]{2,1,0:T(8,128)} %get-tuple-element.660, f32[3,256,256]{2,1,0:T(8,128)S(1)} %copy.59, s32[]{:T(128)} %constant.100.clone.1..sunk.1, s32[]{:T(128)S(6)} %select_n.65, s32[]{:T(128)S(6)} %select_n.66) | dynamic-update-slice | bytes 1572868 | tf_op jit(solution)/shard_map/while/body/eval_jaxpr/dynamic_update_slice | solution.py:114
  547.4 9.4 %dynamic_update_slice.23 = f32[3,512,1024]{2,1,0:T(8,128)} dynamic-update-slice(f32[3,512,1024]{2,1,0:T(8,128)} %get-tuple-element.660, f32[3,256,256]{2,1,0:T(8,128)S(1)} %copy.59, s32[]{:T(128)} %constant.100.clone.1..sunk.1, s32[]{:T(128)S(6)} %select_n.65, s32[]{:T(128)S(6)} %select_n.66) | dynamic-update-slice | bytes 1572868 | tf_op jit(solution)/shard_map/while/body/eval_jaxpr/dynamic_update_slice | solution.py:114
  559.0 5.0 collective-permute-start.3
  566.0 4.8 convert_add_fusion
  570.9 59.1 %all-reduce.3.cloned.1.call-done = (f32[2,2,256,256]{3,2,1,0:T(8,128)}, f32[256,256]{0,1:T(8,128)}) async-done(((f32[2,2,256,256]{3,2,1,0:T(8,128)}, f32[256,256]{0,1:T(8,128)}), (f32[2,2,256,256]{3,2,1,0:T(8,128)}, f32[256,256]{0,1:T(8,128)})) %all-reduce.3.cloned.1.call-update) | async-done | bytes 1310736 | tf_op jit(solution)/shard_map/psum | solution.py:132
  633.4 58.5 %reduce-scatter.2.cloned.1.call-done = f32[3,256,256]{2,1,0:T(8,128)} async-done(((f32[3,256,1024]{2,1,0:T(8,128)}), f32[3,256,256]{2,1,0:T(8,128)}) %reduce-scatter.2.cloned.1.call-update) | async-done | bytes 786448 | tf_op jit(solution)/shard_map/reduce_scatter | solution.py:129
  (335 shorter events, 256.3 us)
Async XLA Ops:
  7.2 5.7 copy-start.7
  7.2 58.4 %all-gather.2.cloned.1.call-start = ((), (), s32[]{:S(2)}) async-start(), calls=%async_computation.1 | async-start | bytes 2621440 | tf_op jit(solution)/shard_map/all_gather | solution.py:47
  8.3 8.3 %copy-start.6 = (f32[2,2,256,256]{3,2,1,0:T(8,128)S(1)}, f32[2,2,256,256]{3,2,1,0:T(8,128)}, u32[]{:S(2)}) copy-start(f32[2,2,256,256]{3,2,1,0:T(8,128)} %param.14) | copy-start | bytes 3145732
  8.3 3.6 collective-permute-start
  12.7 617.2 %all-reduce.3.cloned.1.call-start = ((), (), s32[]{:S(2)}) async-start(), calls=%async_computation.3 | async-start | bytes 2621440 | tf_op jit(solution)/shard_map/psum | solution.py:132
  136.7 52.0 %copy-start.5 = (f32[2,1,256,256]{3,2,1,0:T(8,128)S(1)}, f32[2,1,256,256]{3,2,1,0:T(8,128)}, u32[]{:S(2)}) copy-start(f32[2,1,256,256]{3,2,1,0:T(8,128)} %get-tuple-element.352) | copy-start | bytes 1572868
  136.7 53.0 %copy-start.4 = (f32[2,1,256,256]{3,2,1,0:T(8,128)S(1)}, f32[2,1,256,256]{3,2,1,0:T(8,128)}, u32[]{:S(2)}) copy-start(f32[2,1,256,256]{3,2,1,0:T(8,128)} %get-tuple-element.355) | copy-start | bytes 1572868
  136.8 46.0 %collective-permute-start.1 = (f32[8,256,256]{2,1,0:T(8,128)}, f32[8,256,256]{2,1,0:T(8,128)S(1)}, u32[]{:S(2)}, u32[]{:S(2)}) collective-permute-start(f32[8,256,256]{2,1,0:T(8,128)} %get-tuple-element.155), channel_id=1, source_target_pairs={{0,1},{1,0},{2,3},{3,2},{4,5},{5,4},{6,7},{7,6},{8,9},{9,8},{10,11... | collective-permute-start | bytes 6291464 | tf_op jit(solution)/shard_map/ppermute | solution.py:83
  184.8 92.6 %collective-permute-start.2 = (f32[8,256,256]{2,1,0:T(8,128)S(1)}, f32[8,256,256]{2,1,0:T(8,128)}, u32[]{:S(2)}, u32[]{:S(2)}) collective-permute-start(f32[8,256,256]{2,1,0:T(8,128)S(1)} %add.118), channel_id=1, source_target_pairs={{0,2},{1,3},{2,0},{3,1},{4,6},{5,7},{6,4},{7,5},{8,10},{9,11},{10,... | collective-permute-start | bytes 6291464 | tf_op jit(solution)/shard_map/ppermute | solution.py:83
  304.7 1.5 copy-start.2
  337.1 1.5 copy-start.2
  338.6 1.0 copy-start
  369.9 1.5 copy-start.2
  371.5 1.0 copy-start
  404.8 1.5 copy-start.2
  406.3 1.0 copy-start
  438.9 1.5 copy-start.2
  473.2 1.5 copy-start.2
  507.9 1.5 copy-start.2
  542.5 1.5 copy-start.2
  556.8 7.2 %copy-start.1 = (f32[2,2,256,256]{2,3,0,1:T(8,128)S(1)}, f32[2,2,256,256]{2,3,0,1:T(8,128)}, u32[]{:S(2)}) copy-start(f32[2,2,256,256]{2,3,0,1:T(8,128)} %get-tuple-element.159) | copy-start | bytes 3145732
  559.0 7.0 collective-permute-start.3
  565.3 126.5 %reduce-scatter.2.cloned.1.call-start = ((), (), s32[]{:S(2)}) async-start(), calls=%async_computation.2 | async-start | bytes 3932160 | tf_op jit(solution)/shard_map/reduce_scatter | solution.py:129
  570.9 121.9 %copy-start.3 = (f32[2,256,256]{2,1,0:T(8,128)S(1)}, f32[2,256,256]{2,1,0:T(8,128)}, u32[]{:S(2)}) copy-start(f32[2,256,256]{2,1,0:T(8,128)} %param.13) | copy-start | bytes 1572868
  (5 other events, 5.2 us)
Sparse Core Ops, SparseCore 0:
  12.8 52.6 all-gather.1
  565.4 64.4 all-reduce.2
  632.3 59.5 reduce-scatter.1
